TPU v7x, 256 devices: a whole 4x4x8 slice. The times are simulated.
256 devices in a mesh: gx: 8 (over z_lo, y), gy: 8 (over x, core), dir: 4 (over z_hi).
Axes of the slice: x: 4, y: 4, z: 8 (z_hi: 4, z_lo: 2; z = z_hi * 2 + z_lo), core: 2. Of those that a mesh axis runs over, the one named last changes fastest.
Arguments:
- directions: float32 [32, 1024, 2048], P('dir', 'gx', 'gy'), may hold values from -6 to 6
- velocity: float32 [2, 1024, 2048], P(None, 'gx', 'gy'), may hold values from -6 to 6
- viscosity: float32 [1024, 2048], P('gx', 'gy'), may hold values from 0.5 to 2
- basal_drag: float32 [1024, 2048], P('gx', 'gy'), may hold values from 0.5 to 8
- misfit_weight: float32 [1024, 2048], P('gx', 'gy'), may hold values from 1 to 10
- ice_mask: int32 [1024, 2048], P('gx', 'gy'), may hold values 0 or 1
- grounded: int32 [1024, 2048], P('gx', 'gy'), may hold values 0 or 1
Outputs:
- basis: float32 [32, 1024, 2048], P('dir', 'gx', 'gy')
- upper: float32 [32, 32], replicated
All inputs are finite; a program needn't handle non-finite values. No bound on the sum of `ice_mask` or of `grounded` on one device may be relied on, other than what follows from the above.
Results may differ from a plain program's by a relative error of at most 0.00021.
Values sent between devices are 32-bit elements; how exact they have to be, the bound alone decides.
A program may use at most 64 MiB of HBM per device.

v0:
```python
import jax
import jax.numpy as jnp
from jax import lax
from jax.sharding import PartitionSpec as P

SWEEPS = 6


damping = 0.8


def with_halo(value, sides, width):
    for axis, dim in sides:
        count, length = (lax.axis_size(axis), value.shape[dim])
        up = [(i, (i + 1) % count) for i in range(count - 1)]
        down = [(j, i) for i, j in up]
        last = lax.slice_in_dim(value, length - width, length, axis=dim)
        first = lax.slice_in_dim(value, 0, width, axis=dim)
        before = lax.ppermute(last, axis, up)
        after = lax.ppermute(first, axis, down)
        value = jnp.concatenate([before, value, after], axis=dim)
    return value


def weights_pair():
    along_x = jnp.array([4.0, 1.0], jnp.float32).reshape(2, 1, 1)
    along_y = jnp.array([1.0, 4.0], jnp.float32).reshape(2, 1, 1)
    return (along_x, along_y)


def relax_sweep(state, padded, coeffs, source):
    face_east, face_west, face_north, face_south, friction, diagonal, ice_keep = coeffs
    along_x, along_y = weights_pair()
    next_row = padded[..., 2:, 1:-1]
    prev_row = padded[..., :-2, 1:-1]
    next_col = padded[..., 1:-1, 2:]
    prev_col = padded[..., 1:-1, :-2]
    applied = along_x * (face_east * (state - next_row) + face_west * (state - prev_row))
    applied = applied + along_y * (
        face_north * (state - next_col) + face_south * (state - prev_col)
    )
    applied = applied + friction * state
    return ice_keep * (state + damping * (source - applied) / diagonal)


def solve_shared(source, coeffs):
    diagonal, ice_keep = (coeffs[5], coeffs[6])
    state = ice_keep * damping * source / diagonal
    for sweep in range(SWEEPS - 1):
        padded = with_halo(state, (("gx", 2), ("gy", 3)), 1)
        state = relax_sweep(state, padded, coeffs, source)
    return state


def make_coeffs(viscosity, padded_visc, basal_drag, grounded_f):
    face_east = 0.5 * (viscosity + padded_visc[2:, 1:-1])
    face_west = 0.5 * (viscosity + padded_visc[:-2, 1:-1])
    face_north = 0.5 * (viscosity + padded_visc[1:-1, 2:])
    face_south = 0.5 * (viscosity + padded_visc[1:-1, :-2])
    friction = basal_drag * grounded_f
    along_x, along_y = weights_pair()
    diagonal = along_x * (face_east + face_west) + along_y * (face_north + face_south) + friction
    return (face_east, face_west, face_north, face_south, friction, diagonal)


def on_device(directions, velocity, viscosity, basal_drag, misfit_weight, ice_mask, grounded):
    own_count = directions.shape[0]
    tile_rows = directions.shape[1]
    tile_cols = directions.shape[2]
    padded_visc = with_halo(viscosity, (("gx", 0), ("gy", 1)), 1)
    ice_keep = ice_mask.astype(jnp.float32)
    face_east, face_west, face_north, face_south, friction, diagonal = make_coeffs(
        viscosity, padded_visc, basal_drag, grounded.astype(jnp.float32)
    )
    coeffs = (face_east, face_west, face_north, face_south, friction, diagonal, ice_keep)
    forward = solve_shared(-friction * velocity[None] * directions[:, None], coeffs)
    adjoint = solve_shared(misfit_weight * forward, coeffs)
    sketch = -friction * jnp.sum(velocity[None] * adjoint, axis=1)
    cells = tile_rows * tile_cols
    total_cells = cells * lax.axis_size("gx") * lax.axis_size("gy")
    own_flat = sketch.reshape(own_count, cells)
    identity = jnp.eye(own_count * lax.axis_size("dir"), dtype=jnp.float32)
    whole = lax.all_gather(own_flat, "dir", axis=0, tiled=True)
    gram_local = jnp.dot(
        whole, whole.T, precision=lax.Precision.HIGHEST, preferred_element_type=jnp.float32
    )
    gram_sum = lax.psum(gram_local, ("gx", "gy"))
    lower = jnp.linalg.cholesky(gram_sum / jnp.float32(total_cells))
    inverse = lax.linalg.triangular_solve(lower, identity, left_side=True, lower=True)
    own_rows = lax.dynamic_slice_in_dim(inverse, lax.axis_index("dir") * own_count, own_count, 0)
    basis_flat = jnp.dot(
        own_rows, whole, precision=lax.Precision.HIGHEST, preferred_element_type=jnp.float32
    )
    return (basis_flat.reshape(own_count, tile_rows, tile_cols), lower.T)


def solution(mesh):
    placed = (
        P("dir", "gx", "gy"),
        P(None, "gx", "gy"),
        P("gx", "gy"),
        P("gx", "gy"),
        P("gx", "gy"),
        P("gx", "gy"),
        P("gx", "gy"),
    )
    return jax.shard_map(
        on_device,
        mesh=mesh,
        in_specs=placed,
        out_specs=(P("dir", "gx", "gy"), P()),
        check_vma=False,
    )
```

profile of v0, /device:TPU:64, one launch (start us, length us, event | category | flops | bytes accessed | tf_op | source)
XLA Modules:
  0.0 741.2 jit_solution(18365183644680429997)
XLA Ops:
  9.3 4.5 collective-permute-start.1
  17.9 3.0 collective-permute-start.3
  25.3 4.5 collective-permute-start.5
  33.4 1.9 copy.100
  37.2 3.0 collective-permute-start.7
  44.3 7.2 fusion.4
  52.8 5.0 collective-permute-start.9
  61.5 2.5 copy.104
  65.2 2.5 copy.106
  67.7 4.8 collective-permute-start.11
  72.6 2.4 copy.105
  74.9 2.3 copy.107
  77.2 5.3 fusion.8
  83.9 4.8 collective-permute-start.13
  92.3 2.6 copy.108
  96.3 2.5 copy.110
  98.7 4.1 collective-permute-start.15
  102.9 2.4 copy.109
  105.3 2.4 copy.111
  107.6 5.3 fusion.12
  114.2 6.7 collective-permute-start.17
  124.6 2.6 copy.112
  128.5 2.5 copy.114
  131.0 3.6 collective-permute-start.19
  134.6 2.4 copy.113
  137.0 2.4 copy.115
  139.4 5.3 fusion.16
  146.0 6.9 collective-permute-start.21
  156.5 1.9 copy.116
  160.3 3.0 collective-permute-start.23
  166.7 8.1 %multiply_divide_fusion = (f32[8,2,128,256]{3,0,2,1:T(8,128)S(1)}, f32[8,2,128,256]{3,0,2,1:T(8,128)S(1)}) fusion(f32[2,128,256]{2,1,0:T(8,128)S(1)} %get-tuple-element.69, f32[128,256]{1,0:T(8,128)} %copy-done.17, f32[8,2,128,256]{3,0,2,1:T(8,128)} %copy-done.9, f32[128,256]{1,0:T(8,128)S(1)} %get-tuple-element.11, ...), kind=kLoop, calls=%fused_computation.279 | loop fusion | flops 16777216 | bytes 8962320 | tf_op jit(solution)/shard_map/div | solution.py:48
  176.1 6.7 collective-permute-start.25
  186.2 1.9 copy.120
  189.4 1.9 copy.122
  191.3 3.6 collective-permute-start.27
  198.2 7.3 fusion.182
  206.9 6.9 collective-permute-start.29
  217.1 1.9 copy.124
  220.3 1.9 copy.126
  222.2 4.0 collective-permute-start.31
  229.5 7.0 fusion.183
  237.8 6.7 collective-permute-start.33
  247.8 1.9 copy.128
  251.0 1.9 copy.130
  252.8 3.8 collective-permute-start.35
  260.0 7.0 fusion.184
  268.3 6.9 collective-permute-start.37
  278.5 1.9 copy.132
  281.9 1.9 copy.134
  283.8 4.0 collective-permute-start.39
  291.2 7.0 fusion.185
  299.5 6.9 collective-permute-start.41
  310.1 2.5 copy.136
  313.9 2.5 copy.138
  316.4 4.6 collective-permute-start.43
  322.0 2.4 copy.137
  324.3 2.4 copy.139
  326.7 7.1 multiply_reduce_fusion
  335.0 99.5 %all-gather.2.cloned.1.call-done = f32[32,32768]{1,0:T(8,128)} async-done(((f32[8,32768]{1,0:T(8,128)}), f32[32,32768]{1,0:T(8,128)}) %all-gather.2.cloned.1.call-update) | async-done | bytes 4194320 | tf_op jit(solution)/shard_map/all_gather | solution.py:83
  434.4 6.9 fusion.230
  441.4 279.7 %psum.7 = f32[32,32]{0,1:T(8,128)S(1)} all-reduce(f32[32,32]{0,1:T(8,128)S(1)} %fusion.230), channel_id=1, replica_groups=mesh['gx'=8,'gy'=8,'dir'=4] {'gx','gy'}, use_global_device_ids=true, to_apply=%region_1.0 | all-reduce | flops 1024 | bytes 8192 | tf_op jit(solution)/shard_map/psum | solution.py:87
  721.2 2.9 cholesky.17
  725.4 2.4 custom-call.6
  728.1 3.8 fusion.198
  (200 shorter events, 97.6 us)
Async XLA Ops:
  7.2 15.4 %copy-start.21 = (f32[128,256]{1,0:T(8,128)S(1)}, f32[128,256]{1,0:T(8,128)}, u32[]{:S(2)}) copy-start(f32[128,256]{1,0:T(8,128)} %param.31) | copy-start | bytes 393220
  7.2 14.7 %copy-start.18 = (f32[8,128,256]{2,1,0:T(8,128)S(1)}, f32[8,128,256]{2,1,0:T(8,128)}, u32[]{:S(2)}) copy-start(f32[8,128,256]{2,1,0:T(8,128)} %param.29) | copy-start | bytes 3145732
  7.2 427.3 %all-gather.2.cloned.1.call-start = ((), (), s32[]{:S(2)}) async-start(), calls=%async_computation | async-start | bytes 5242880 | tf_op jit(solution)/shard_map/all_gather | solution.py:83
  8.0 7.5 %collective-permute-start = (f32[1,256]{1,0:T(1,128)S(1)}, f32[1,256]{1,0:T(1,128)S(1)}, u32[]{:S(2)}, u32[]{:S(2)}) collective-permute-start(f32[1,256]{1,0:T(1,128)S(1)} %get-tuple-element.66), channel_id=1, source_target_pairs={{32,0},{64,32},{96,64},{128,96},{160,128},{192,160},{224,192},{33,... | collective-permute-start | bytes 3080 | tf_op jit(solution)/shard_map/ppermute | solution.py:20
  9.3 6.2 collective-permute-start.1
  16.6 5.9 collective-permute-start.2
  17.9 4.6 collective-permute-start.3
  24.0 5.9 collective-permute-start.4
  25.3 6.0 collective-permute-start.5
  35.3 5.7 collective-permute-start.6
  37.2 5.4 collective-permute-start.7
  51.5 6.3 collective-permute-start.8
  52.8 6.4 collective-permute-start.9
  64.0 8.6 %collective-permute-start.10 = (f32[8,2,130,1]{2,0,3,1:T(8,128)}, f32[8,2,130,1]{2,0,3,1:T(8,128)}, u32[]{:S(2)}, u32[]{:S(2)}) collective-permute-start(f32[8,2,130,1]{2,0,3,1:T(8,128)} %copy.104), channel_id=1, source_target_pairs={{4,0},{8,4},{12,8},{16,12},{20,16},{24,20},{28,24},{5,1},{9,5},{13... | collective-permute-start | bytes 24968 | tf_op jit(solution)/shard_map/ppermute | solution.py:20
  67.7 7.2 collective-permute-start.11
  82.6 6.1 collective-permute-start.12
  83.9 6.2 collective-permute-start.13
  92.3 15.3 %copy-start.2 = (f32[8,2,128,256]{3,0,2,1:T(8,128)S(1)}, f32[8,2,128,256]{3,0,2,1:T(8,128)}, u32[]{:S(2)}) copy-start(f32[8,2,128,256]{3,0,2,1:T(8,128)} %copy-done.1) | copy-start | bytes 6291460
  95.0 7.9 %collective-permute-start.14 = (f32[8,2,130,1]{2,0,3,1:T(8,128)}, f32[8,2,130,1]{2,0,3,1:T(8,128)}, u32[]{:S(2)}, u32[]{:S(2)}) collective-permute-start(f32[8,2,130,1]{2,0,3,1:T(8,128)} %copy.108), channel_id=1, source_target_pairs={{4,0},{8,4},{12,8},{16,12},{20,16},{24,20},{28,24},{5,1},{9,5},{13... | collective-permute-start | bytes 24968 | tf_op jit(solution)/shard_map/ppermute | solution.py:20
  98.7 6.5 collective-permute-start.15
  112.9 9.6 %copy-start.3 = (f32[8,2,128,256]{3,0,2,1:T(8,128)}, f32[8,2,128,256]{3,0,2,1:T(8,128)S(1)}, u32[]{:S(2)}) copy-start(f32[8,2,128,256]{3,0,2,1:T(8,128)S(1)} %fusion.12) | copy-start | bytes 6291460
  112.9 8.0 %collective-permute-start.16 = (f32[8,2,1,256]{3,0,2,1:T(8,128)S(1)}, f32[8,2,1,256]{3,0,2,1:T(8,128)S(1)}, u32[]{:S(2)}, u32[]{:S(2)}) collective-permute-start(f32[8,2,1,256]{3,0,2,1:T(8,128)S(1)} %get-tuple-element.53), channel_id=1, source_target_pairs={{32,0},{64,32},{96,64},{128,96},{160,128},{192,160},{224,192},{33,... | collective-permute-start | bytes 49160 | tf_op jit(solution)/shard_map/ppermute | solution.py:20
  114.2 8.1 %collective-permute-start.17 = (f32[8,2,1,256]{3,0,2,1:T(8,128)S(1)}, f32[8,2,1,256]{3,0,2,1:T(8,128)S(1)}, u32[]{:S(2)}, u32[]{:S(2)}) collective-permute-start(f32[8,2,1,256]{3,0,2,1:T(8,128)S(1)} %get-tuple-element.52), channel_id=1, source_target_pairs={{0,32},{32,64},{64,96},{96,128},{128,160},{160,192},{192,224},{1,3... | collective-permute-start | bytes 49160 | tf_op jit(solution)/shard_map/ppermute | solution.py:19
  124.6 14.8 %copy-start.4 = (f32[8,2,128,256]{3,0,2,1:T(8,128)S(1)}, f32[8,2,128,256]{3,0,2,1:T(8,128)}, u32[]{:S(2)}) copy-start(f32[8,2,128,256]{3,0,2,1:T(8,128)} %copy-done.3) | copy-start | bytes 6291460
  127.2 7.4 collective-permute-start.18
  131.0 6.0 collective-permute-start.19
  144.7 10.4 %copy-start.9 = (f32[8,2,128,256]{3,0,2,1:T(8,128)}, f32[8,2,128,256]{3,0,2,1:T(8,128)S(1)}, u32[]{:S(2)}) copy-start(f32[8,2,128,256]{3,0,2,1:T(8,128)S(1)} %fusion.16) | copy-start | bytes 6291460
  144.7 8.2 %collective-permute-start.20 = (f32[8,2,1,256]{3,0,2,1:T(8,128)S(1)}, f32[8,2,1,256]{3,0,2,1:T(8,128)S(1)}, u32[]{:S(2)}, u32[]{:S(2)}) collective-permute-start(f32[8,2,1,256]{3,0,2,1:T(8,128)S(1)} %get-tuple-element.51), channel_id=1, source_target_pairs={{32,0},{64,32},{96,64},{128,96},{160,128},{192,160},{224,192},{33,... | collective-permute-start | bytes 49160 | tf_op jit(solution)/shard_map/ppermute | solution.py:20
  146.0 8.4 %collective-permute-start.21 = (f32[8,2,1,256]{3,0,2,1:T(8,128)S(1)}, f32[8,2,1,256]{3,0,2,1:T(8,128)S(1)}, u32[]{:S(2)}, u32[]{:S(2)}) collective-permute-start(f32[8,2,1,256]{3,0,2,1:T(8,128)S(1)} %get-tuple-element.50), channel_id=1, source_target_pairs={{0,32},{32,64},{64,96},{96,128},{128,160},{160,192},{192,224},{1,3... | collective-permute-start | bytes 49160 | tf_op jit(solution)/shard_map/ppermute | solution.py:19
  158.3 5.0 collective-permute-start.22
  160.3 4.7 collective-permute-start.23
  174.8 9.6 %copy-start.10 = (f32[8,2,128,256]{3,0,2,1:T(8,128)}, f32[8,2,128,256]{3,0,2,1:T(8,128)S(1)}, u32[]{:S(2)}) copy-start(f32[8,2,128,256]{3,0,2,1:T(8,128)S(1)} %get-tuple-element.12) | copy-start | bytes 6291460
  174.8 8.0 %collective-permute-start.24 = (f32[8,2,1,256]{3,0,2,1:T(8,128)S(1)}, f32[8,2,1,256]{3,0,2,1:T(8,128)S(1)}, u32[]{:S(2)}, u32[]{:S(2)}) collective-permute-start(f32[8,2,1,256]{3,0,2,1:T(8,128)S(1)} %get-tuple-element.49), channel_id=1, source_target_pairs={{32,0},{64,32},{96,64},{128,96},{160,128},{192,160},{224,192},{33,... | collective-permute-start | bytes 49160 | tf_op jit(solution)/shard_map/ppermute | solution.py:20
  176.1 8.1 %collective-permute-start.25 = (f32[8,2,1,256]{3,0,2,1:T(8,128)S(1)}, f32[8,2,1,256]{3,0,2,1:T(8,128)S(1)}, u32[]{:S(2)}, u32[]{:S(2)}) collective-permute-start(f32[8,2,1,256]{3,0,2,1:T(8,128)S(1)} %get-tuple-element.48), channel_id=1, source_target_pairs={{0,32},{32,64},{64,96},{96,128},{128,160},{160,192},{192,224},{1,3... | collective-permute-start | bytes 49160 | tf_op jit(solution)/shard_map/ppermute | solution.py:19
  186.1 12.1 %copy-start.11 = (f32[128,256]{1,0:T(8,128)S(1)}, f32[128,256]{1,0:T(8,128)}, u32[]{:S(2)}) copy-start(f32[128,256]{1,0:T(8,128)} %convert_element_type.8) | copy-start | bytes 393220
  186.1 12.1 %copy-start.12 = (f32[128,256]{1,0:T(8,128)S(1)}, f32[128,256]{1,0:T(8,128)}, u32[]{:S(2)}) copy-start(f32[128,256]{1,0:T(8,128)} %get-tuple-element.15) | copy-start | bytes 393220
  186.1 12.1 %copy-start.13 = (f32[128,256]{1,0:T(8,128)S(1)}, f32[128,256]{1,0:T(8,128)}, u32[]{:S(2)}) copy-start(f32[128,256]{1,0:T(8,128)} %get-tuple-element.16) | copy-start | bytes 393220
  186.1 12.1 %copy-start.14 = (f32[128,256]{1,0:T(8,128)S(1)}, f32[128,256]{1,0:T(8,128)}, u32[]{:S(2)}) copy-start(f32[128,256]{1,0:T(8,128)} %get-tuple-element.63) | copy-start | bytes 393220
  186.1 12.1 %copy-start.15 = (f32[128,256]{1,0:T(8,128)S(1)}, f32[128,256]{1,0:T(8,128)}, u32[]{:S(2)}) copy-start(f32[128,256]{1,0:T(8,128)} %get-tuple-element.64) | copy-start | bytes 393220
  186.1 12.1 %copy-start.30 = (f32[2]{0:T(128)S(1)}, f32[2]{0:T(128)}, u32[]{:S(2)}) copy-start(f32[2]{0:T(128)} %constant.63.clone) | copy-start | bytes 28
  186.2 12.1 %copy-start.32 = (f32[2]{0:T(128)S(1)}, f32[2]{0:T(128)}, u32[]{:S(2)}) copy-start(f32[2]{0:T(128)} %constant.64.clone) | copy-start | bytes 28
  188.1 6.8 collective-permute-start.26
  191.3 5.3 collective-permute-start.27
  205.6 9.8 %copy-start.5 = (f32[8,2,128,256]{3,0,2,1:T(8,128)}, f32[8,2,128,256]{3,0,2,1:T(8,128)S(1)}, u32[]{:S(2)}) copy-start(f32[8,2,128,256]{3,0,2,1:T(8,128)S(1)} %fusion.182) | copy-start | bytes 6291460
  205.6 8.2 %collective-permute-start.28 = (f32[8,2,1,256]{3,0,2,1:T(8,128)S(1)}, f32[8,2,1,256]{3,0,2,1:T(8,128)S(1)}, u32[]{:S(2)}, u32[]{:S(2)}) collective-permute-start(f32[8,2,1,256]{3,0,2,1:T(8,128)S(1)} %get-tuple-element.47), channel_id=1, source_target_pairs={{32,0},{64,32},{96,64},{128,96},{160,128},{192,160},{224,192},{33,... | collective-permute-start | bytes 49160 | tf_op jit(solution)/shard_map/ppermute | solution.py:20
  206.9 8.4 %collective-permute-start.29 = (f32[8,2,1,256]{3,0,2,1:T(8,128)S(1)}, f32[8,2,1,256]{3,0,2,1:T(8,128)S(1)}, u32[]{:S(2)}, u32[]{:S(2)}) collective-permute-start(f32[8,2,1,256]{3,0,2,1:T(8,128)S(1)} %get-tuple-element.46), channel_id=1, source_target_pairs={{0,32},{32,64},{64,96},{96,128},{128,160},{160,192},{192,224},{1,3... | collective-permute-start | bytes 49160 | tf_op jit(solution)/shard_map/ppermute | solution.py:19
  219.0 7.2 collective-permute-start.30
  222.2 5.7 collective-permute-start.31
  236.5 9.6 %copy-start.6 = (f32[8,2,128,256]{3,0,2,1:T(8,128)}, f32[8,2,128,256]{3,0,2,1:T(8,128)S(1)}, u32[]{:S(2)}) copy-start(f32[8,2,128,256]{3,0,2,1:T(8,128)S(1)} %fusion.183) | copy-start | bytes 6291460
  236.6 8.0 %collective-permute-start.32 = (f32[8,2,1,256]{3,0,2,1:T(8,128)S(1)}, f32[8,2,1,256]{3,0,2,1:T(8,128)S(1)}, u32[]{:S(2)}, u32[]{:S(2)}) collective-permute-start(f32[8,2,1,256]{3,0,2,1:T(8,128)S(1)} %get-tuple-element.45), channel_id=1, source_target_pairs={{32,0},{64,32},{96,64},{128,96},{160,128},{192,160},{224,192},{33,... | collective-permute-start | bytes 49160 | tf_op jit(solution)/shard_map/ppermute | solution.py:20
  237.8 8.1 %collective-permute-start.33 = (f32[8,2,1,256]{3,0,2,1:T(8,128)S(1)}, f32[8,2,1,256]{3,0,2,1:T(8,128)S(1)}, u32[]{:S(2)}, u32[]{:S(2)}) collective-permute-start(f32[8,2,1,256]{3,0,2,1:T(8,128)S(1)} %get-tuple-element.44), channel_id=1, source_target_pairs={{0,32},{32,64},{64,96},{96,128},{128,160},{160,192},{192,224},{1,3... | collective-permute-start | bytes 49160 | tf_op jit(solution)/shard_map/ppermute | solution.py:19
  249.7 7.0 collective-permute-start.34
  252.8 5.5 collective-permute-start.35
  267.0 9.8 %copy-start.7 = (f32[8,2,128,256]{3,0,2,1:T(8,128)}, f32[8,2,128,256]{3,0,2,1:T(8,128)S(1)}, u32[]{:S(2)}) copy-start(f32[8,2,128,256]{3,0,2,1:T(8,128)S(1)} %fusion.184) | copy-start | bytes 6291460
  267.0 8.2 %collective-permute-start.36 = (f32[8,2,1,256]{3,0,2,1:T(8,128)S(1)}, f32[8,2,1,256]{3,0,2,1:T(8,128)S(1)}, u32[]{:S(2)}, u32[]{:S(2)}) collective-permute-start(f32[8,2,1,256]{3,0,2,1:T(8,128)S(1)} %get-tuple-element.43), channel_id=1, source_target_pairs={{32,0},{64,32},{96,64},{128,96},{160,128},{192,160},{224,192},{33,... | collective-permute-start | bytes 49160 | tf_op jit(solution)/shard_map/ppermute | solution.py:20
  268.3 8.4 %collective-permute-start.37 = (f32[8,2,1,256]{3,0,2,1:T(8,128)S(1)}, f32[8,2,1,256]{3,0,2,1:T(8,128)S(1)}, u32[]{:S(2)}, u32[]{:S(2)}) collective-permute-start(f32[8,2,1,256]{3,0,2,1:T(8,128)S(1)} %get-tuple-element.42), channel_id=1, source_target_pairs={{0,32},{32,64},{64,96},{96,128},{128,160},{160,192},{192,224},{1,3... | collective-permute-start | bytes 49160 | tf_op jit(solution)/shard_map/ppermute | solution.py:19
  280.4 7.4 collective-permute-start.38
  283.8 5.7 collective-permute-start.39
  298.2 9.8 %copy-start = (f32[8,2,128,256]{3,0,2,1:T(8,128)}, f32[8,2,128,256]{3,0,2,1:T(8,128)S(1)}, u32[]{:S(2)}) copy-start(f32[8,2,128,256]{3,0,2,1:T(8,128)S(1)} %fusion.185) | copy-start | bytes 6291460
  298.2 8.2 %collective-permute-start.40 = (f32[8,2,1,256]{3,0,2,1:T(8,128)S(1)}, f32[8,2,1,256]{3,0,2,1:T(8,128)S(1)}, u32[]{:S(2)}, u32[]{:S(2)}) collective-permute-start(f32[8,2,1,256]{3,0,2,1:T(8,128)S(1)} %get-tuple-element.41), channel_id=1, source_target_pairs={{32,0},{64,32},{96,64},{128,96},{160,128},{192,160},{224,192},{33,... | collective-permute-start | bytes 49160 | tf_op jit(solution)/shard_map/ppermute | solution.py:20
  299.5 8.4 %collective-permute-start.41 = (f32[8,2,1,256]{3,0,2,1:T(8,128)S(1)}, f32[8,2,1,256]{3,0,2,1:T(8,128)S(1)}, u32[]{:S(2)}, u32[]{:S(2)}) collective-permute-start(f32[8,2,1,256]{3,0,2,1:T(8,128)S(1)} %get-tuple-element.40), channel_id=1, source_target_pairs={{0,32},{32,64},{64,96},{96,128},{128,160},{160,192},{192,224},{1,3... | collective-permute-start | bytes 49160 | tf_op jit(solution)/shard_map/ppermute | solution.py:19
  310.1 16.6 %copy-start.20 = (f32[2,128,256]{2,1,0:T(8,128)S(1)}, f32[2,128,256]{2,1,0:T(8,128)}, u32[]{:S(2)}) copy-start(f32[2,128,256]{2,1,0:T(8,128)} %param.30) | copy-start | bytes 786436
  312.6 9.3 %collective-permute-start.42 = (f32[8,2,130,1]{2,0,3,1:T(8,128)}, f32[8,2,130,1]{2,0,3,1:T(8,128)}, u32[]{:S(2)}, u32[]{:S(2)}) collective-permute-start(f32[8,2,130,1]{2,0,3,1:T(8,128)} %copy.136), channel_id=1, source_target_pairs={{4,0},{8,4},{12,8},{16,12},{20,16},{24,20},{28,24},{5,1},{9,5},{13... | collective-permute-start | bytes 24968 | tf_op jit(solution)/shard_map/ppermute | solution.py:20
  316.4 7.9 %collective-permute-start.43 = (f32[8,2,130,1]{2,0,3,1:T(8,128)}, f32[8,2,130,1]{2,0,3,1:T(8,128)}, u32[]{:S(2)}, u32[]{:S(2)}) collective-permute-start(f32[8,2,130,1]{2,0,3,1:T(8,128)} %copy.138), channel_id=1, source_target_pairs={{0,4},{4,8},{8,12},{12,16},{16,20},{20,24},{24,28},{1,5},{5,9},{9,... | collective-permute-start | bytes 24968 | tf_op jit(solution)/shard_map/ppermute | solution.py:19
  (14 other events, 60.3 us)
Sparse Core Ops, SparseCore 0:
  335.1 99.3 all-gather.1
where the time goes:
time: 752 us; the launch traced here: 741 us
  blocking collectives  280 us (37%)
  starting transfers between devices  137 us (18%)
  waiting for transfers between devices  114 us (15%)
  local copies, waits for them, and re-layouts  103 us (14%)
  other arithmetic  81.4 us (11%)
  between operations  15.5 us (2%)
  matrix products  11 us (1%)
    psum x1, blocking collectives, on_device(): gram_sum = lax.psum(gram_local, ('gx', 'gy'))  280 us
    ppermute x22, starting transfers between devices, with_halo(): before = lax.ppermute(last, axis, up)  108 us
    all_gather x1, waiting for transfers between devices, on_device(): whole = lax.all_gather(own_flat, 'dir', axis=0, tiled=True)  99.5 us
    mul x8, other arithmetic, relax_sweep(): return ice_keep * (state + damping * (source - applied) / diagonal)  51.3 us
    slice x21, local copies, waits for them, and re-layouts, with_halo(): first = lax.slice_in_dim(value, 0, width, axis=dim)  37.7 us
    ppermute x22, starting transfers between devices, with_halo(): after = lax.ppermute(first, axis, down)  28.6 us
    slice x21, local copies, waits for them, and re-layouts, with_halo(): last = lax.slice_in_dim(value, length - width, length, axis=dim)  19.6 us
    ppermute x10, local copies, waits for them, and re-layouts, with_halo(): after = lax.ppermute(first, axis, down)  19.5 us
  transfers between devices with their start and end apart: 45, of which 11 were waited for; matrix products, arithmetic and copies ran while one was open for 6% of the time, Pallas kernels for 0%

commit v1 on v0

v1 whole, which is shorter than its diff:
```python
import functools

import jax
import jax.numpy as jnp
from jax import lax
from jax.experimental import pallas as pl
from jax.experimental.pallas import tpu as pltpu
from jax.sharding import PartitionSpec as P

SWEEPS = 6
DAMPING = 0.8
HR = 16
HC = 16
AX = (4.0, 1.0)
AY = (1.0, 4.0)
LEVELS = 2 * (SWEEPS - 1)
CHUNKS = 4
MESH = pl.DeviceIdType.MESH
F32 = jnp.float32
BF16 = jnp.bfloat16
VEL, VISC, FRIC, MISFIT, KEEP = 0, 2, 3, 4, 5
CE, CW, CN, CS, SB, GM, CQ = range(0, 14, 2)


def split(x):
    hi = x.astype(BF16)
    lo = (x - hi.astype(F32)).astype(BF16)
    return hi, lo


def dot(a, b, contract):
    return lax.dot_general(a, b, ((contract[:1], contract[1:]), ((), ())), preferred_element_type=F32)


def kernel(
    sizes,
    dirs_hbm,
    vel_hbm,
    visc_hbm,
    drag_hbm,
    misfit_hbm,
    mask_hbm,
    ground_hbm,
    out_hbm,
    upper_ref,
    fld,
    fldc,
    dr,
    drc,
    raw,
    rawi,
    pks,
    pkr,
    co,
    w,
    sk,
    rx,
    gs,
    gr,
    ob,
    in_sem,
    row_send,
    row_recv,
    col_send,
    col_recv,
    a2a_send,
    a2a_recv,
    own_sem,
    ar_send,
    ar_recv,
    ret_send,
    ret_recv,
    ret_own,
):
    gx_n, gy_n, nd, rows, total = sizes
    full = rows + 2 * HR
    blocks = full // 8
    chunk = rows // CHUNKS
    quarter = chunk // nd
    kk = 8 * nd
    gx, gy, me = (lax.axis_index(a) for a in ("gx", "gy", "dir"))
    lane = lax.broadcasted_iota(jnp.int32, (8, 128), 1)

    barrier = pltpu.get_barrier_semaphore()
    peers = 0
    for axis, index, count in (("gx", gx, gx_n), ("gy", gy, gy_n), ("dir", me, nd)):
        for o in range(1, count):
            pl.semaphore_signal(
                barrier, inc=1, device_id={axis: lax.rem(index + o, count)}, device_id_type=MESH
            )
            peers += 1

    dr4 = dr.reshape(2, 8, full, 128)
    body = pl.ds(HR, rows)
    loads = []
    for t in range(2):
        cols = pl.ds(128 * t, 128)
        loads += [
            (vel_hbm.at[:, :, cols], fld.at[0:2, t, body, :]),
            (visc_hbm.at[:, cols], fld.at[VISC, t, body, :]),
            (misfit_hbm.at[:, cols], fld.at[MISFIT, t, body, :]),
            (drag_hbm.at[:, cols], raw.at[t]),
            (mask_hbm.at[:, cols], rawi.at[0, t]),
            (ground_hbm.at[:, cols], rawi.at[1, t]),
            (dirs_hbm.at[:, :, cols], dr4.at[t, :, body, :]),
        ]
    copies = [pltpu.make_async_copy(s, d, in_sem.at[i]) for i, (s, d) in enumerate(loads)]
    for c in copies:
        c.start()

    def zero_rows(start):
        z = jnp.zeros((HR, 128), F32)
        for t in range(2):
            for p in range(6):
                fld[p, t, pl.ds(start, HR), :] = z
            for k in range(8):
                dr[t, pl.ds(k * full + start, HR), :] = z

    @pl.when(gx == 0)
    def _():
        zero_rows(0)

    @pl.when(gx == gx_n - 1)
    def _():
        zero_rows(HR + rows)

    @pl.when(gy == 0)
    def _():
        pkr[:, 0] = jnp.zeros((2, full, 128), F32)

    @pl.when(gy == gy_n - 1)
    def _():
        pkr[:, 1] = jnp.zeros((2, full, 128), F32)

    for c in copies:
        c.wait()
    for t in range(2):
        fld[FRIC, t, body, :] = raw[t] * rawi[1, t].astype(F32)
        fld[KEEP, t, body, :] = rawi[0, t].astype(F32)
    pl.semaphore_wait(barrier, peers)

    top, bottom = pl.ds(HR, HR), pl.ds(rows, HR)
    above, below = pl.ds(0, HR), pl.ds(HR + rows, HR)

    def row_copy(kind, up):
        src, dst = (top, below) if up else (bottom, above)
        ref = (fld, dr4)[kind]
        peer = lax.rem(gx + (gx_n - 1 if up else 1), gx_n)
        return pltpu.make_async_remote_copy(
            src_ref=ref.at[:, :, src, :],
            dst_ref=ref.at[:, :, dst, :],
            send_sem=row_send.at[kind, int(up)],
            recv_sem=row_recv.at[kind, int(up)],
            device_id={"gx": peer},
            device_id_type=MESH,
        )

    has_up, has_down = gx > 0, gx < gx_n - 1
    for kind in range(2):

        @pl.when(has_up)
        def _():
            row_copy(kind, True).start()

        @pl.when(has_down)
        def _():
            row_copy(kind, False).start()

    def col_copy(kind, left):
        peer = lax.rem(gy + (gy_n - 1 if left else 1), gy_n)
        return pltpu.make_async_remote_copy(
            src_ref=pks.at[kind, 0 if left else 1],
            dst_ref=pkr.at[kind, 1 if left else 0],
            send_sem=col_send.at[kind, int(left)],
            recv_sem=col_recv.at[kind, int(left)],
            device_id={"gy": peer},
            device_id_type=MESH,
        )

    has_left, has_right = gy > 0, gy < gy_n - 1

    def plane(kind, p, t, at):
        if kind == 0:
            return fld[p, t, at, :]
        return dr[t, pl.ds(pl.multiple_of(p * full + at.start, 8), 8), :]

    for kind in range(2):
        count = (6, 8)[kind]

        @pl.when(has_down)
        def _():
            row_copy(kind, True).wait_recv()

        @pl.when(has_up)
        def _():
            row_copy(kind, False).wait_recv()

        def pack(i, _):
            at = pl.ds(pl.multiple_of(8 * i, 8), 8)
            to_left = jnp.zeros((8, 128), F32)
            to_right = jnp.zeros((8, 128), F32)
            for p in range(count):
                here = (lane >= HC * p) & (lane < HC * (p + 1))
                first = plane(kind, p, 0, at)
                last = plane(kind, p, 1, at)
                if p:
                    first = pltpu.roll(first, HC * p, axis=1)
                if p != 7:
                    last = pltpu.roll(last, (HC * p - (128 - HC)) % 128, axis=1)
                to_left = jnp.where(here, first, to_left)
                to_right = jnp.where(here, last, to_right)
            pks[kind, 0, at, :] = to_left
            pks[kind, 1, at, :] = to_right
            return 0

        lax.fori_loop(0, blocks, pack, 0)

        @pl.when(has_left)
        def _():
            col_copy(kind, True).start()

        @pl.when(has_right)
        def _():
            col_copy(kind, False).start()

    def unpack(kind):
        count = (6, 8)[kind]

        @pl.when(has_right)
        def _():
            col_copy(kind, True).wait_recv()

        @pl.when(has_left)
        def _():
            col_copy(kind, False).wait_recv()

        def one(i, _):
            at = pl.ds(pl.multiple_of(8 * i, 8), 8)
            left = pkr[kind, 0, at, :]
            right = pkr[kind, 1, at, :]
            for p in range(count):
                r = right if p == 0 else pltpu.roll(right, 128 - HC * p, axis=1)
                l = left if p == 7 else pltpu.roll(left, 128 - HC * (p + 1), axis=1)
                v = jnp.where(lane < HC, r, jnp.where(lane >= 128 - HC, l, 0.0))
                if kind == 0:
                    fldc[p, at, :] = v
                else:
                    drc[pl.ds(pl.multiple_of(p * full + 8 * i, 8), 8), :] = v
            return 0

        lax.fori_loop(0, blocks, one, 0)

    unpack(0)

    def around(tiles):
        nxt = [pltpu.roll(x, 127, axis=1) for x in tiles]
        prv = [pltpu.roll(x, 1, axis=1) for x in tiles]
        after = [jnp.where(lane == 127, nxt[(t + 1) % 3], nxt[t]) for t in range(3)]
        before = [jnp.where(lane == 0, prv[(t + 2) % 3], prv[t]) for t in range(3)]
        return before, after

    def coefficients(i, _):
        at = pl.ds(pl.multiple_of(8 * i, 8), 8)
        at_up = pl.ds(pl.multiple_of(8 * lax.rem(i + blocks - 1, blocks), 8), 8)
        at_down = pl.ds(pl.multiple_of(8 * lax.rem(i + 1, blocks), 8), 8)

        def field(p, rows_at):
            return [fld[p, 0, rows_at, :], fld[p, 1, rows_at, :], fldc[p, rows_at, :]]

        sub = lax.broadcasted_iota(jnp.int32, (8, 128), 0)
        visc = field(VISC, at)
        up, down = field(VISC, at_up), field(VISC, at_down)
        before, after = around(visc)
        fric, misfit, keep = field(FRIC, at), field(MISFIT, at), field(KEEP, at)
        vel = [field(VEL, at), field(VEL + 1, at)]
        for t in range(3):
            v = visc[t]
            below_row = jnp.where(sub == 7, pltpu.roll(down[t], 7, axis=0), pltpu.roll(v, 7, axis=0))
            above_row = jnp.where(sub == 0, pltpu.roll(up[t], 1, axis=0), pltpu.roll(v, 1, axis=0))
            east, west = 0.5 * (v + below_row), 0.5 * (v + above_row)
            north, south = 0.5 * (v + after[t]), 0.5 * (v + before[t])
            for c in range(2):
                diagonal = AX[c] * (east + west) + AY[c] * (north + south) + fric[t]
                g = (DAMPING * keep[t]) / jnp.where(keep[t] > 0.0, diagonal, 1.0)
                gx_, gy_ = AX[c] * g, AY[c] * g
                q = -fric[t] * vel[c][t]
                co[CE + c, t, at, :] = gx_ * east
                co[CW + c, t, at, :] = gx_ * west
                co[CN + c, t, at, :] = gy_ * north
                co[CS + c, t, at, :] = gy_ * south
                co[SB + c, t, at, :] = g * q
                co[GM + c, t, at, :] = g * misfit[t]
                co[CQ + c, t, at, :] = q
        return 0

    lax.fori_loop(0, blocks, coefficients, 0)
    unpack(1)

    def coef(p, t, r):
        return jnp.broadcast_to(co[p, t, pl.ds(r, 1), :], (8, 128))

    def first_level(r):
        for t in range(3):
            d = (dr[t, pl.ds(r, 8, stride=full), :] if t < 2 else drc[pl.ds(r, 8, stride=full), :])
            for c in range(2):
                w[0, r, 3 * c + t] = coef(SB + c, t, r) * d

    def level_rows(level, r0, count):
        local = (level - 1) % (SWEEPS - 1) + 1
        src = 0 if local == 1 else 1 + local % 2
        dst = 1 + (local + 1) % 2
        last = level == LEVELS
        half = local == SWEEPS - 1 and not last
        tiles = range(2) if last else range(3)
        sums = [[None, None] for _ in range(count)]
        for c in range(2):
            state = [[w[src, r0 + j, 3 * c + t] for t in range(3)] for j in range(-1, count + 1)]
            for j in range(count):
                r = r0 + j
                up, here, down = state[j], state[j + 1], state[j + 2]
                before, after = around(here)
                for t in tiles:
                    new = 0.2 * here[t] + w[0, r, 3 * c + t]
                    new = new + coef(CE + c, t, r) * down[t] + coef(CW + c, t, r) * up[t]
                    new = new + (coef(CN + c, t, r) * after[t] + coef(CS + c, t, r) * before[t])
                    if last:
                        term = coef(CQ + c, t, r) * new
                        sums[j][t] = term if c == 0 else sums[j][t] + term
                    elif half:
                        w[0, r, 3 * c + t] = coef(GM + c, t, r) * new
                    else:
                        w[dst, r, 3 * c + t] = new
        if last:
            for j in range(count):
                for t in range(2):
                    sk[r0 + j - HR, t] = sums[j][t]

    def a2a_copy(c, o):
        peer = lax.rem(me + o, nd)
        return pltpu.make_async_remote_copy(
            src_ref=sk.at[pl.ds(c * chunk + peer * quarter, quarter)],
            dst_ref=rx.at[me, pl.ds(c * quarter, quarter)],
            send_sem=a2a_send.at[c, o],
            recv_sem=a2a_recv.at[c, o],
            device_id={"dir": peer},
            device_id_type=MESH,
        )

    def own_copy(c):
        return pltpu.make_async_copy(
            sk.at[pl.ds(c * chunk + me * quarter, quarter)],
            rx.at[me, pl.ds(c * quarter, quarter)],
            own_sem.at[c],
        )

    base = HR + LEVELS

    def do_chunk(c, _):
        first = 1 - (c + CHUNKS) // (CHUNKS + 1)
        for level in range(LEVELS + 1):
            stop = base - level + chunk * c
            lo = stop - chunk + first * (chunk - 2 * LEVELS + 2 * level)

            def step(i, _):
                if level == 0:
                    first_level(lo + 2 * i)
                    first_level(lo + 2 * i + 1)
                else:
                    level_rows(level, lo + 2 * i, 2)
                return 0

            lax.fori_loop(0, (stop - lo) // 2, step, 0)

        @pl.when(c > 0)
        def _():
            for o in range(1, nd):
                a2a_copy(c - 1, o).start()
            own_copy(c - 1).start()

        return 0

    lax.fori_loop(0, CHUNKS + 1, do_chunk, 0)

    def gathered(r):
        return [
            jnp.concatenate([rx[g, r, t] for g in range(nd)], axis=0) for t in range(2)
        ]

    def gram_chunk(c, acc):
        for o in range(1, nd):
            a2a_copy(c, o).wait_recv()
        own_copy(c).wait()

        def one(i, acc):
            for x in gathered(c * quarter + i):
                hi, lo = split(x)
                both = jnp.concatenate([hi, lo], axis=0)
                acc = acc + dot(both, both, (1, 1))
            return acc

        return lax.fori_loop(0, quarter, one, acc)

    acc = lax.fori_loop(0, CHUNKS, gram_chunk, jnp.zeros((2 * kk, 2 * kk), F32))
    acc = acc[:kk] + acc[kk:]
    gram = acc[:, :kk] + acc[:, kk:]
    gram = jnp.concatenate([gram, jnp.zeros((kk, 128 - kk), F32)], axis=1)

    def reduce_copy(s, axis, index, count, o):
        return pltpu.make_async_remote_copy(
            src_ref=gs.at[s],
            dst_ref=gr.at[s, index],
            send_sem=ar_send.at[s, o],
            recv_sem=ar_recv.at[s, o],
            device_id={axis: lax.rem(index + o, count)},
            device_id_type=MESH,
        )

    for s, (axis, index, count) in enumerate((("dir", me, nd), ("gy", gy, gy_n), ("gx", gx, gx_n))):
        gs[s] = gram
        gr[s, index] = gram
        for o in range(1, count):
            reduce_copy(s, axis, index, count, o).start()
        for o in range(1, count):
            reduce_copy(s, axis, index, count, o).wait_recv()
        gram = gr[s, 0]
        for j in range(1, count):
            gram = gram + gr[s, j]
    gram = gram / jnp.float32(total)

    line = lax.broadcasted_iota(jnp.int32, (kk, 128), 0)
    place = lax.broadcasted_iota(jnp.int32, (kk, 128), 1)
    m = jnp.where(place == line + kk, 1.0, gram)
    for k in range(kk - 1):
        column = jnp.broadcast_to(m[:, k : k + 1], (kk, 128))
        row = jnp.broadcast_to(m[k : k + 1, :], (kk, 128))
        pivot = jnp.broadcast_to(column[k : k + 1, :], (kk, 128))
        m = m - jnp.where(line > k, column, 0.0) * (row / pivot)
    diag = jnp.sum(jnp.where(place == line, m, 0.0), axis=1, keepdims=True)
    m = m * lax.rsqrt(diag)
    upper_ref[...] = jnp.where(place >= line, m, 0.0)[:, :kk]
    inverse = m[:, kk : 2 * kk]
    inv_hi, inv_lo = split(inverse)
    left = jnp.concatenate(
        [jnp.concatenate([inv_hi, inv_hi], axis=1), jnp.concatenate([inv_lo, inv_lo], axis=1)], axis=0
    )

    def ret_copy(c, o):
        peer = lax.rem(me + o, nd)
        return pltpu.make_async_remote_copy(
            src_ref=ob.at[peer, c],
            dst_ref=out_hbm.at[:, :, pl.ds(c * chunk + me * quarter, quarter), :],
            send_sem=ret_send.at[c, o],
            recv_sem=ret_recv.at[c, o],
            device_id={"dir": peer},
            device_id_type=MESH,
        )

    def ret_own_copy(c):
        return pltpu.make_async_copy(
            ob.at[me, c],
            out_hbm.at[:, :, pl.ds(c * chunk + me * quarter, quarter), :],
            ret_own.at[c],
        )

    def basis_chunk(c, _):
        def one(i, _):
            for t, x in enumerate(gathered(c * quarter + i)):
                hi, lo = split(x)
                out = dot(left, jnp.concatenate([hi, lo], axis=0), (1, 0))
                out = out[:kk] + out[kk:]
                for g in range(nd):
                    flat = ob.at[g, c, t].reshape(8 * quarter, 128)
                    flat[pl.ds(i, 8, stride=quarter), :] = out[8 * g : 8 * g + 8]
            return 0

        lax.fori_loop(0, quarter, one, 0)
        for o in range(1, nd):
            ret_copy(c, o).start()
        ret_own_copy(c).start()
        return 0

    lax.fori_loop(0, CHUNKS, basis_chunk, 0)

    for kind in range(2):

        @pl.when(has_up)
        def _():
            row_copy(kind, True).wait_send()

        @pl.when(has_down)
        def _():
            row_copy(kind, False).wait_send()

        @pl.when(has_left)
        def _():
            col_copy(kind, True).wait_send()

        @pl.when(has_right)
        def _():
            col_copy(kind, False).wait_send()

    for s, (axis, index, count) in enumerate((("dir", me, nd), ("gy", gy, gy_n), ("gx", gx, gx_n))):
        for o in range(1, count):
            reduce_copy(s, axis, index, count, o).wait_send()

    def finish(c, _):
        for o in range(1, nd):
            a2a_copy(c, o).wait_send()
            ret_copy(c, o).wait_send()
            ret_copy(c, o).wait_recv()
        ret_own_copy(c).wait()
        return 0

    lax.fori_loop(0, CHUNKS, finish, 0)


def on_device(mesh, directions, velocity, viscosity, basal_drag, misfit_weight, ice_mask, grounded):
    gx_n, gy_n, nd = (mesh.shape[a] for a in ("gx", "gy", "dir"))
    own, rows, cols = directions.shape
    full = rows + 2 * HR
    chunk = rows // CHUNKS
    quarter = chunk // nd
    kk = own * nd
    total = rows * cols * gx_n * gy_n
    most = max(gx_n, gy_n, nd)
    any_space = pl.BlockSpec(memory_space=pl.ANY)
    dma = pltpu.SemaphoreType.DMA
    vmem = pltpu.VMEM
    out, upper = pl.pallas_call(
        functools.partial(kernel, (gx_n, gy_n, nd, rows, total)),
        out_shape=(
            jax.ShapeDtypeStruct((2, own, rows, 128), F32),
            jax.ShapeDtypeStruct((kk, kk), F32),
        ),
        in_specs=[any_space] * 7,
        out_specs=(any_space, pl.BlockSpec(memory_space=pltpu.VMEM)),
        scratch_shapes=[
            vmem((6, 2, full, 128), F32),
            vmem((6, full, 128), F32),
            vmem((2, 8 * full, 128), F32),
            vmem((8 * full, 128), F32),
            vmem((2, rows, 128), F32),
            vmem((2, 2, rows, 128), jnp.int32),
            vmem((2, 2, full, 128), F32),
            vmem((2, 2, full, 128), F32),
            vmem((14, 3, full, 128), F32),
            vmem((3, full, 6, 8, 128), F32),
            vmem((rows, 2, 8, 128), F32),
            vmem((nd, rows // nd, 2, 8, 128), F32),
            vmem((3, kk, 128), F32),
            vmem((3, most, kk, 128), F32),
            vmem((nd, CHUNKS, 2, 8, quarter, 128), F32),
            dma((14,)),
            dma((2, 2)),
            dma((2, 2)),
            dma((2, 2)),
            dma((2, 2)),
            dma((CHUNKS, nd)),
            dma((CHUNKS, nd)),
            dma((CHUNKS,)),
            dma((3, most)),
            dma((3, most)),
            dma((CHUNKS, nd)),
            dma((CHUNKS, nd)),
            dma((CHUNKS,)),
        ],
        compiler_params=pltpu.CompilerParams(
            collective_id=0, has_side_effects=True, vmem_limit_bytes=48 << 20
        ),
        name="sketch",
    )(directions, velocity, viscosity, basal_drag, misfit_weight, ice_mask, grounded)
    return out.transpose(1, 2, 0, 3).reshape(own, rows, cols), upper


def solution(mesh):
    placed = (P("dir", "gx", "gy"), P(None, "gx", "gy")) + (P("gx", "gy"),) * 5
    return jax.shard_map(
        functools.partial(on_device, mesh),
        mesh=mesh,
        in_specs=placed,
        out_specs=(P("dir", "gx", "gy"), P()),
        check_vma=False,
    )
```

time: 752 us -> 157 us (0.21); the launches traced: 741 us -> 156 us
  blocking collectives: 280 us -> 0 us
  Pallas kernels: 0 us -> 147 us
  starting transfers between devices: 137 us -> 0 us
  waiting for transfers between devices: 114 us -> 0 us
  local copies, waits for them, and re-layouts: 103 us -> 8.93 us
  other arithmetic: 81.4 us -> 0 us
  between operations: 15.5 us -> 0.66 us
  matrix products: 11 us -> 0 us
    psum x1 -> x0, blocking collectives: 280 us -> none  [on_device(): gram_sum = lax.psum(gram_local, ('gx', 'gy'))]
    pallas_call x0 -> x1, Pallas kernels: none -> 147 us  [on_device(): pl.pallas_call(functools.partial(kernel, (gx_n, gy_n, nd, rows, total)),...]
    ppermute x44 -> x0, starting transfers between devices: 137 us -> none  [the longest x22 108 us: with_halo(): before = lax.ppermute(last, axis, up)]
    all_gather x1 -> x0, waiting for transfers between devices: 99.5 us -> none  [on_device(): whole = lax.all_gather(own_flat, 'dir', axis=0, tiled=True)]
    slice x42 -> x0, local copies, waits for them, and re-layouts: 57.3 us -> none  [the longest x21 37.7 us: with_halo(): first = lax.slice_in_dim(value, 0, width, axis=dim)]
    mul x10 -> x0, other arithmetic: 53.3 us -> none  [the longest x8 51.3 us: relax_sweep(): return ice_keep * (state + damping * (source - applied) / diagonal)]
    ppermute x20 -> x0, local copies, waits for them, and re-layouts: 39 us -> none  [the longest x10 19.5 us: with_halo(): after = lax.ppermute(first, axis, down)]
    ppermute x44 -> x0, waiting for transfers between devices: 14.2 us -> none  [the longest x22 14.2 us: with_halo(): before = lax.ppermute(last, axis, up)]
  transfers between devices with their start and end apart: 45 -> 0, of which waited for: 11 -> 0; matrix products, arithmetic and copies ran while one was open for 6% -> 0% of each run, Pallas kernels for 0% -> 0%
where the time goes in v1:
time: 157 us; the launch traced here: 156 us
  Pallas kernels  147 us (94%)
  local copies, waits for them, and re-layouts  8.93 us (6%)
    pallas_call x1, Pallas kernels, on_device(): pl.pallas_call(functools.partial(kernel, (gx_n, gy_n, nd, rows, total)),...  147 us
    unnamed x16, local copies, waits for them, and re-layouts  8.6 us

profile of v1, /device:TPU:64, one launch (start us, length us, event | category | flops | bytes accessed | tf_op | source)
XLA Modules:
  0.0 156.2 jit_solution(5377966823401479018)
XLA Ops:
  0.6 0.0 copy-start
  0.6 1.2 copy-done
  1.9 0.0 copy-start.1
  1.9 0.9 copy-done.1
  2.8 0.0 copy-start.2
  2.8 0.9 copy-done.2
  3.7 0.0 copy-start.3
  3.7 0.9 copy-done.3
  4.6 0.0 copy-start.4
  4.6 0.9 copy-done.4
  5.5 0.0 copy-start.5
  5.5 0.9 copy-done.5
  6.4 0.0 copy-start.6
  6.4 0.9 copy-done.6
  7.3 146.6 %sketch.1 = (f32[2,8,128,128]{3,2,1,0:T(8,128)S(1)}, f32[32,32]{1,0:T(8,128)S(1)}) custom-call(f32[8,128,256]{2,1,0:T(8,128)S(1)} %copy-done, f32[2,128,256]{2,1,0:T(8,128)S(1)} %copy-done.1, f32[128,256]{1,0:T(8,128)S(1)} %copy-done.2, f32[128,256]{1,0:T(8,128)S(1)} %copy-done.3, f32[128,256]{1,0:T(8,128)S(1)} %copy-done.4, s32[128,256]{1,0:T(8,128)S(1)} %copy-done.5, ...), custom_call_target="tpu_custom_call" | custom-call | tf_op jit(solution)/shard_map/sketch/pallas_call | solution.py:529
  153.9 0.3 copy.9
  154.3 1.3 copy.10
  155.6 0.6 copy.12
Async XLA Ops:
  0.6 1.2 copy-start
  1.9 0.9 copy-start.1
  2.8 0.9 copy-start.2
  3.7 0.9 copy-start.3
  4.6 0.9 copy-start.4
  5.5 0.9 copy-start.5
  6.4 0.9 copy-start.6

commit v2 on v1

--- a/solution.py
+++ b/solution.py
@@ -15,6 +15,7 @@
 AY = (1.0, 4.0)
 LEVELS = 2 * (SWEEPS - 1)
 CHUNKS = 4
+STEP = 8
 MESH = pl.DeviceIdType.MESH
 F32 = jnp.float32
 BF16 = jnp.bfloat16
@@ -213,7 +214,7 @@
             pks[kind, 1, at, :] = to_right
             return 0
 
-        lax.fori_loop(0, blocks, pack, 0)
+        lax.fori_loop(0, blocks // 4, lambda i, x: [pack(4 * i + j, x) for j in range(4)][0], 0)
 
         @pl.when(has_left)
         def _():
@@ -248,7 +249,7 @@
                     drc[pl.ds(pl.multiple_of(p * full + 8 * i, 8), 8), :] = v
             return 0
 
-        lax.fori_loop(0, blocks, one, 0)
+        lax.fori_loop(0, blocks // 4, lambda i, x: [one(4 * i + j, x) for j in range(4)][0], 0)
 
     unpack(0)
 
@@ -293,7 +294,7 @@
                 co[CQ + c, t, at, :] = q
         return 0
 
-    lax.fori_loop(0, blocks, coefficients, 0)
+    lax.fori_loop(0, blocks // 2, lambda i, x: [coefficients(2 * i + j, x) for j in range(2)][0], 0)
     unpack(1)
 
     def coef(p, t, r):
@@ -359,17 +360,18 @@
         first = 1 - (c + CHUNKS) // (CHUNKS + 1)
         for level in range(LEVELS + 1):
             stop = base - level + chunk * c
-            lo = stop - chunk + first * (chunk - 2 * LEVELS + 2 * level)
+            early = -(-2 * (LEVELS - level) // STEP) * STEP
+            lo = stop - chunk + first * (chunk - early)
 
             def step(i, _):
                 if level == 0:
-                    first_level(lo + 2 * i)
-                    first_level(lo + 2 * i + 1)
+                    for j in range(STEP):
+                        first_level(lo + STEP * i + j)
                 else:
-                    level_rows(level, lo + 2 * i, 2)
+                    level_rows(level, lo + STEP * i, STEP)
                 return 0
 
-            lax.fori_loop(0, (stop - lo) // 2, step, 0)
+            lax.fori_loop(0, (stop - lo) // STEP, step, 0)
 
         @pl.when(c > 0)
         def _():
@@ -381,24 +383,21 @@
 
     lax.fori_loop(0, CHUNKS + 1, do_chunk, 0)
 
-    def gathered(r):
-        return [
-            jnp.concatenate([rx[g, r, t] for g in range(nd)], axis=0) for t in range(2)
-        ]
+    def gathered(c):
+        parts = []
+        for i in range(quarter):
+            for t in range(2):
+                x = [rx[g, c * quarter + i, t] for g in range(nd)]
+                parts.append(jnp.concatenate(split(jnp.concatenate(x, axis=0)), axis=0))
+        return jnp.concatenate(parts, axis=1)
 
     def gram_chunk(c, acc):
         for o in range(1, nd):
             a2a_copy(c, o).wait_recv()
         own_copy(c).wait()
 
-        def one(i, acc):
-            for x in gathered(c * quarter + i):
-                hi, lo = split(x)
-                both = jnp.concatenate([hi, lo], axis=0)
-                acc = acc + dot(both, both, (1, 1))
-            return acc
-
-        return lax.fori_loop(0, quarter, one, acc)
+        both = gathered(c)
+        return acc + dot(both, both, (1, 1))
 
     acc = lax.fori_loop(0, CHUNKS, gram_chunk, jnp.zeros((2 * kk, 2 * kk), F32))
     acc = acc[:kk] + acc[kk:]
@@ -444,39 +443,37 @@
         [jnp.concatenate([inv_hi, inv_hi], axis=1), jnp.concatenate([inv_lo, inv_lo], axis=1)], axis=0
     )
 
-    def ret_copy(c, o):
+    def ret_copy(c, o, t):
         peer = lax.rem(me + o, nd)
         return pltpu.make_async_remote_copy(
-            src_ref=ob.at[peer, c],
-            dst_ref=out_hbm.at[:, :, pl.ds(c * chunk + me * quarter, quarter), :],
-            send_sem=ret_send.at[c, o],
-            recv_sem=ret_recv.at[c, o],
+            src_ref=ob.at[peer, c, t],
+            dst_ref=out_hbm.at[:, pl.ds(c * chunk + me * quarter, quarter), pl.ds(128 * t, 128)],
+            send_sem=ret_send.at[c, o, t],
+            recv_sem=ret_recv.at[c, o, t],
             device_id={"dir": peer},
             device_id_type=MESH,
         )
 
-    def ret_own_copy(c):
+    def ret_own_copy(c, t):
         return pltpu.make_async_copy(
-            ob.at[me, c],
-            out_hbm.at[:, :, pl.ds(c * chunk + me * quarter, quarter), :],
-            ret_own.at[c],
+            ob.at[me, c, t],
+            out_hbm.at[:, pl.ds(c * chunk + me * quarter, quarter), pl.ds(128 * t, 128)],
+            ret_own.at[c, t],
         )
 
     def basis_chunk(c, _):
-        def one(i, _):
-            for t, x in enumerate(gathered(c * quarter + i)):
-                hi, lo = split(x)
-                out = dot(left, jnp.concatenate([hi, lo], axis=0), (1, 0))
-                out = out[:kk] + out[kk:]
+        whole = dot(left, gathered(c), (1, 0))
+        whole = whole[:kk] + whole[kk:]
+        for i in range(quarter):
+            for t in range(2):
+                out = whole[:, 128 * (2 * i + t) : 128 * (2 * i + t + 1)]
                 for g in range(nd):
                     flat = ob.at[g, c, t].reshape(8 * quarter, 128)
                     flat[pl.ds(i, 8, stride=quarter), :] = out[8 * g : 8 * g + 8]
-            return 0
-
-        lax.fori_loop(0, quarter, one, 0)
-        for o in range(1, nd):
-            ret_copy(c, o).start()
-        ret_own_copy(c).start()
+        for t in range(2):
+            for o in range(1, nd):
+                ret_copy(c, o, t).start()
+            ret_own_copy(c, t).start()
         return 0
 
     lax.fori_loop(0, CHUNKS, basis_chunk, 0)
@@ -506,9 +503,11 @@
     def finish(c, _):
         for o in range(1, nd):
             a2a_copy(c, o).wait_send()
-            ret_copy(c, o).wait_send()
-            ret_copy(c, o).wait_recv()
-        ret_own_copy(c).wait()
+            for t in range(2):
+                ret_copy(c, o, t).wait_send()
+                ret_copy(c, o, t).wait_recv()
+        for t in range(2):
+            ret_own_copy(c, t).wait()
         return 0
 
     lax.fori_loop(0, CHUNKS, finish, 0)
@@ -526,10 +525,10 @@
     any_space = pl.BlockSpec(memory_space=pl.ANY)
     dma = pltpu.SemaphoreType.DMA
     vmem = pltpu.VMEM
-    out, upper = pl.pallas_call(
+    return pl.pallas_call(
         functools.partial(kernel, (gx_n, gy_n, nd, rows, total)),
         out_shape=(
-            jax.ShapeDtypeStruct((2, own, rows, 128), F32),
+            jax.ShapeDtypeStruct((own, rows, cols), F32),
             jax.ShapeDtypeStruct((kk, kk), F32),
         ),
         in_specs=[any_space] * 7,
@@ -560,16 +559,15 @@
             dma((CHUNKS,)),
             dma((3, most)),
             dma((3, most)),
-            dma((CHUNKS, nd)),
-            dma((CHUNKS, nd)),
-            dma((CHUNKS,)),
+            dma((CHUNKS, nd, 2)),
+            dma((CHUNKS, nd, 2)),
+            dma((CHUNKS, 2)),
         ],
         compiler_params=pltpu.CompilerParams(
-            collective_id=0, has_side_effects=True, vmem_limit_bytes=48 << 20
+            collective_id=0, has_side_effects=True, vmem_limit_bytes=62 << 20
         ),
         name="sketch",
     )(directions, velocity, viscosity, basal_drag, misfit_weight, ice_mask, grounded)
-    return out.transpose(1, 2, 0, 3).reshape(own, rows, cols), upper
 
 
 def solution(mesh):

time: 157 us -> 110 us (0.70)
  Pallas kernels: 147 us -> 107 us
  local copies, waits for them, and re-layouts: 8.93 us -> 2.88 us
    pallas_call x1, Pallas kernels: 147 us -> 107 us  [on_device(): pl.pallas_call(functools.partial(kernel, (gx_n, gy_n, nd, rows, total)),...]
    unnamed x16 -> x4, local copies, waits for them, and re-layouts: 8.6 us -> 2.88 us
where the time goes in v2:
time: 110 us
  Pallas kernels  107 us (97%)
  local copies, waits for them, and re-layouts  2.88 us (3%)
    pallas_call x1, Pallas kernels, on_device(): pl.pallas_call(functools.partial(kernel, (gx_n, gy_n, nd, rows, total)),...  107 us
    unnamed x4, local copies, waits for them, and re-layouts  2.88 us

profile of v2, /device:TPU:64, one launch (start us, length us, event | category | flops | bytes accessed | tf_op | source)
XLA Modules:
  0.0 110.1 jit_solution(11433211033753035725)
XLA Ops:
  0.6 106.6 %sketch.1 = (f32[8,128,256]{2,1,0:T(8,128)}, f32[32,32]{1,0:T(8,128)}) custom-call(f32[8,128,256]{2,1,0:T(8,128)} %dirs_hbm.1, f32[2,128,256]{2,1,0:T(8,128)} %vel_hbm.1, f32[128,256]{1,0:T(8,128)} %visc_hbm.1, f32[128,256]{1,0:T(8,128)} %drag_hbm.1, f32[128,256]{1,0:T(8,128)} %misfit_hbm.1, s32[128,256]{1,0:T(8,128)} %mask_hbm.1, s32[128,256]{1,0:T(8,128)} %ground_hbm.1), custom_call_target="tpu_custom_call" | custom-call | tf_op jit(solution)/shard_map/sketch/pallas_call | solution.py:528
  107.2 0.0 copy-start
  107.2 2.3 %copy.11 = f32[8,128,256]{2,1,0:T(8,128)} copy(f32[8,128,256]{2,1,0:T(8,128)} %get-tuple-element.4) | data formatting | bytes 2097152
  109.5 0.0 copy-done
  109.5 0.6 copy.12
Async XLA Ops:
  107.2 2.3 %copy-start = (f32[32,32]{1,0:T(8,128)S(1)}, f32[32,32]{1,0:T(8,128)}, u32[]{:S(2)}) copy-start(f32[32,32]{1,0:T(8,128)} %get-tuple-element.5) | copy-start | bytes 12292

commit v3 on v2

--- a/solution.py
+++ b/solution.py
@@ -15,7 +15,6 @@
 AY = (1.0, 4.0)
 LEVELS = 2 * (SWEEPS - 1)
 CHUNKS = 4
-STEP = 8
 MESH = pl.DeviceIdType.MESH
 F32 = jnp.float32
 BF16 = jnp.bfloat16
@@ -45,9 +44,13 @@
     out_hbm,
     upper_ref,
     fld,
-    fldc,
     dr,
-    drc,
+    fldp,
+    drp,
+    halves,
+    spread,
+    gather,
+    terms,
     raw,
     rawi,
     pks,
@@ -133,6 +136,20 @@
     def _():
         pkr[:, 1] = jnp.zeros((2, full, 128), F32)
 
+    cols = 256
+    k_in = lax.broadcasted_iota(jnp.int32, (384, 384), 0)
+    k_out = lax.broadcasted_iota(jnp.int32, (384, 384), 1)
+    inside = jnp.where(k_in < cols + HC, k_in + HC, jnp.where(k_in >= 384 - HC, k_in - (384 - HC), -1))
+    third = (k_out % 128) * 3 + k_out // 128
+    there = jnp.where(inside == third, 1.0, 0.0).astype(BF16)
+    spread[0:384] = there
+    spread[384:768] = there
+    k_in = lax.broadcasted_iota(jnp.int32, (384, cols), 0)
+    k_out = lax.broadcasted_iota(jnp.int32, (384, cols), 1)
+    back = jnp.where((k_in % 128) * 3 + k_in // 128 == k_out + HC, 1.0, 0.0).astype(BF16)
+    gather[0:384] = back
+    gather[384:768] = back
+
     for c in copies:
         c.wait()
     for t in range(2):
@@ -236,44 +253,61 @@
             col_copy(kind, False).wait_recv()
 
         def one(i, _):
-            at = pl.ds(pl.multiple_of(8 * i, 8), 8)
+            at = pl.ds(pl.multiple_of(16 * i, 16), 16)
             left = pkr[kind, 0, at, :]
             right = pkr[kind, 1, at, :]
+            lane2 = lax.broadcasted_iota(jnp.int32, (16, 128), 1)
             for p in range(count):
                 r = right if p == 0 else pltpu.roll(right, 128 - HC * p, axis=1)
                 l = left if p == 7 else pltpu.roll(left, 128 - HC * (p + 1), axis=1)
-                v = jnp.where(lane < HC, r, jnp.where(lane >= 128 - HC, l, 0.0))
+                edge = jnp.where(lane2 < HC, r, jnp.where(lane2 >= 128 - HC, l, 0.0))
                 if kind == 0:
-                    fldc[p, at, :] = v
+                    whole = [fld[p, 0, at, :], fld[p, 1, at, :], edge]
                 else:
-                    drc[pl.ds(pl.multiple_of(p * full + 8 * i, 8), 8), :] = v
+                    own = pl.ds(pl.multiple_of(p * full + 16 * i, 16), 16)
+                    whole = [dr[0, own, :], dr[1, own, :], edge]
+                rows_at = pl.ds(pl.multiple_of((6 * kind + p) * full + 16 * i, 16), 16)
+                for t in range(3):
+                    hi, lo = split(whole[t])
+                    halves[rows_at, 128 * t : 128 * t + 128] = hi
+                    halves[rows_at, 384 + 128 * t : 512 + 128 * t] = lo
             return 0
 
-        lax.fori_loop(0, blocks // 4, lambda i, x: [one(4 * i + j, x) for j in range(4)][0], 0)
+        lax.fori_loop(0, full // 32, lambda i, x: [one(2 * i + j, x) for j in range(2)][0], 0)
+        size = 2 * full
+
+        def spread_out(i, _):
+            part = halves[pl.ds(pl.multiple_of(6 * kind * full + i * size, 16), size), :]
+            out = dot(part, spread[...], (1, 0))
+            for t in range(3):
+                ref = (fldp, drp)[kind]
+                ref[t, pl.ds(pl.multiple_of(i * size, 8), size), :] = out[:, 128 * t : 128 * t + 128]
+            return 0
+
+        lax.fori_loop(0, count // 2, spread_out, 0)
 
     unpack(0)
 
     def around(tiles):
-        nxt = [pltpu.roll(x, 127, axis=1) for x in tiles]
-        prv = [pltpu.roll(x, 1, axis=1) for x in tiles]
-        after = [jnp.where(lane == 127, nxt[(t + 1) % 3], nxt[t]) for t in range(3)]
-        before = [jnp.where(lane == 0, prv[(t + 2) % 3], prv[t]) for t in range(3)]
+        before = [pltpu.roll(tiles[2], 1, axis=1), tiles[0], tiles[1]]
+        after = [tiles[1], tiles[2], pltpu.roll(tiles[0], 127, axis=1)]
         return before, after
 
     def coefficients(i, _):
         at = pl.ds(pl.multiple_of(8 * i, 8), 8)
-        at_up = pl.ds(pl.multiple_of(8 * lax.rem(i + blocks - 1, blocks), 8), 8)
-        at_down = pl.ds(pl.multiple_of(8 * lax.rem(i + 1, blocks), 8), 8)
-
-        def field(p, rows_at):
-            return [fld[p, 0, rows_at, :], fld[p, 1, rows_at, :], fldc[p, rows_at, :]]
+        this = 8 * i
+        prev_at = 8 * lax.rem(i + blocks - 1, blocks)
+        next_at = 8 * lax.rem(i + 1, blocks)
+
+        def field(p, start):
+            return [fldp[t, pl.ds(pl.multiple_of(p * full + start, 8), 8), :] for t in range(3)]
 
         sub = lax.broadcasted_iota(jnp.int32, (8, 128), 0)
-        visc = field(VISC, at)
-        up, down = field(VISC, at_up), field(VISC, at_down)
+        visc = field(VISC, this)
+        up, down = field(VISC, prev_at), field(VISC, next_at)
         before, after = around(visc)
-        fric, misfit, keep = field(FRIC, at), field(MISFIT, at), field(KEEP, at)
-        vel = [field(VEL, at), field(VEL + 1, at)]
+        fric, misfit, keep = field(FRIC, this), field(MISFIT, this), field(KEEP, this)
+        vel = [field(VEL, this), field(VEL + 1, this)]
         for t in range(3):
             v = visc[t]
             below_row = jnp.where(sub == 7, pltpu.roll(down[t], 7, axis=0), pltpu.roll(v, 7, axis=0))
@@ -302,7 +336,7 @@
 
     def first_level(r):
         for t in range(3):
-            d = (dr[t, pl.ds(r, 8, stride=full), :] if t < 2 else drc[pl.ds(r, 8, stride=full), :])
+            d = drp[t, pl.ds(r, 8, stride=full), :]
             for c in range(2):
                 w[0, r, 3 * c + t] = coef(SB + c, t, r) * d
 
@@ -312,8 +346,8 @@
         dst = 1 + (local + 1) % 2
         last = level == LEVELS
         half = local == SWEEPS - 1 and not last
-        tiles = range(2) if last else range(3)
-        sums = [[None, None] for _ in range(count)]
+        tiles = range(3)
+        sums = [[None] * 3 for _ in range(count)]
         for c in range(2):
             state = [[w[src, r0 + j, 3 * c + t] for t in range(3)] for j in range(-1, count + 1)]
             for j in range(count):
@@ -333,8 +367,8 @@
                         w[dst, r, 3 * c + t] = new
         if last:
             for j in range(count):
-                for t in range(2):
-                    sk[r0 + j - HR, t] = sums[j][t]
+                for t in range(3):
+                    terms[8 * j : 8 * j + 8, 128 * t : 128 * t + 128] = sums[j][t]
 
     def a2a_copy(c, o):
         peer = lax.rem(me + o, nd)
@@ -354,34 +388,29 @@
             own_sem.at[c],
         )
 
-    base = HR + LEVELS
+    def do_level(level, lo, count):
+        if level == 0:
+            for j in range(count):
+                first_level(lo + j)
+        else:
+            level_rows(level, lo, count)
+
+    for level in range(LEVELS):
+        do_level(level, HR - LEVELS + level, 2 * (LEVELS - level))
 
     def do_chunk(c, _):
-        first = 1 - (c + CHUNKS) // (CHUNKS + 1)
         for level in range(LEVELS + 1):
-            stop = base - level + chunk * c
-            early = -(-2 * (LEVELS - level) // STEP) * STEP
-            lo = stop - chunk + first * (chunk - early)
-
-            def step(i, _):
-                if level == 0:
-                    for j in range(STEP):
-                        first_level(lo + STEP * i + j)
-                else:
-                    level_rows(level, lo + STEP * i, STEP)
-                return 0
-
-            lax.fori_loop(0, (stop - lo) // STEP, step, 0)
-
-        @pl.when(c > 0)
-        def _():
-            for o in range(1, nd):
-                a2a_copy(c - 1, o).start()
-            own_copy(c - 1).start()
-
+            do_level(level, HR + LEVELS - level + chunk * c, chunk)
+        out = dot(jnp.concatenate(split(terms[...]), axis=1), gather[...], (1, 0))
+        for i in range(chunk):
+            for t in range(2):
+                sk[c * chunk + i, t] = out[8 * i : 8 * i + 8, 128 * t : 128 * t + 128]
+        for o in range(1, nd):
+            a2a_copy(c, o).start()
+        own_copy(c).start()
         return 0
 
-    lax.fori_loop(0, CHUNKS + 1, do_chunk, 0)
+    lax.fori_loop(0, CHUNKS, do_chunk, 0)
 
     def gathered(c):
         parts = []
@@ -535,9 +564,13 @@
         out_specs=(any_space, pl.BlockSpec(memory_space=pltpu.VMEM)),
         scratch_shapes=[
             vmem((6, 2, full, 128), F32),
-            vmem((6, full, 128), F32),
             vmem((2, 8 * full, 128), F32),
-            vmem((8 * full, 128), F32),
+            vmem((3, 6 * full, 128), F32),
+            vmem((3, 8 * full, 128), F32),
+            vmem((14 * full, 768), BF16),
+            vmem((768, 384), BF16),
+            vmem((768, cols), BF16),
+            vmem((chunk * own, 384), F32),
             vmem((2, rows, 128), F32),
             vmem((2, 2, rows, 128), jnp.int32),
             vmem((2, 2, full, 128), F32),

time: 110 us -> 100 us (0.909)
  Pallas kernels: 107 us -> 96.1 us
    pallas_call x1, Pallas kernels: 107 us -> 96.1 us  [on_device(): pl.pallas_call(functools.partial(kernel, (gx_n, gy_n, nd, rows, total)),...]
where the time goes in v3:
time: 100 us; the launch traced here: 99.7 us
  Pallas kernels  96.1 us (96%)
  local copies, waits for them, and re-layouts  2.88 us (3%)
    pallas_call x1, Pallas kernels, on_device(): pl.pallas_call(functools.partial(kernel, (gx_n, gy_n, nd, rows, total)),...  96.1 us
    unnamed x4, local copies, waits for them, and re-layouts  2.88 us

profile of v3, /device:TPU:64, one launch (start us, length us, event | category | flops | bytes accessed | tf_op | source)
XLA Modules:
  0.0 99.7 jit_solution(5232124087790711025)
XLA Ops:
  0.6 96.1 %sketch.1 = (f32[8,128,256]{2,1,0:T(8,128)}, f32[32,32]{1,0:T(8,128)}) custom-call(f32[8,128,256]{2,1,0:T(8,128)} %dirs_hbm.1, f32[2,128,256]{2,1,0:T(8,128)} %vel_hbm.1, f32[128,256]{1,0:T(8,128)} %visc_hbm.1, f32[128,256]{1,0:T(8,128)} %drag_hbm.1, f32[128,256]{1,0:T(8,128)} %misfit_hbm.1, s32[128,256]{1,0:T(8,128)} %mask_hbm.1, s32[128,256]{1,0:T(8,128)} %ground_hbm.1), custom_call_target="tpu_custom_call" | custom-call | tf_op jit(solution)/shard_map/sketch/pallas_call | solution.py:557
  96.8 0.0 copy-start
  96.8 2.3 %copy.11 = f32[8,128,256]{2,1,0:T(8,128)} copy(f32[8,128,256]{2,1,0:T(8,128)} %get-tuple-element.4) | data formatting | bytes 2097152
  99.1 0.0 copy-done
  99.1 0.6 copy.12
Async XLA Ops:
  96.8 2.3 %copy-start = (f32[32,32]{1,0:T(8,128)S(1)}, f32[32,32]{1,0:T(8,128)}, u32[]{:S(2)}) copy-start(f32[32,32]{1,0:T(8,128)} %get-tuple-element.5) | copy-start | bytes 12292

commit v4 on v3

--- a/solution.py
+++ b/solution.py
@@ -67,6 +67,8 @@
     row_recv,
     col_send,
     col_recv,
+    corner_send,
+    corner_recv,
     a2a_send,
     a2a_recv,
     own_sem,
@@ -94,6 +96,23 @@
             )
             peers += 1
 
+    corners = [(up, left) for up in (True, False) for left in (True, False)]
+    has_up, has_down = gx > 0, gx < gx_n - 1
+    has_left, has_right = gy > 0, gy < gy_n - 1
+
+    def corner_id(up, left):
+        return {
+            "gx": lax.rem(gx + (gx_n - 1 if up else 1), gx_n),
+            "gy": lax.rem(gy + (gy_n - 1 if left else 1), gy_n),
+        }
+
+    def at_corner(up, left):
+        return (has_up if up else has_down) & (has_left if left else has_right)
+
+    for up, left in corners:
+        pl.semaphore_signal(barrier, inc=1, device_id=corner_id(up, left), device_id_type=MESH)
+        peers += 1
+
     dr4 = dr.reshape(2, 8, full, 128)
     body = pl.ds(HR, rows)
     loads = []
@@ -114,6 +133,7 @@
 
     def zero_rows(start):
         z = jnp.zeros((HR, 128), F32)
+        pkr[:, :, pl.ds(start, HR), :] = jnp.zeros((2, 2, HR, 128), F32)
         for t in range(2):
             for p in range(6):
                 fld[p, t, pl.ds(start, HR), :] = z
@@ -173,7 +193,6 @@
             device_id_type=MESH,
         )
 
-    has_up, has_down = gx > 0, gx < gx_n - 1
     for kind in range(2):
 
         @pl.when(has_up)
@@ -187,15 +206,24 @@
     def col_copy(kind, left):
         peer = lax.rem(gy + (gy_n - 1 if left else 1), gy_n)
         return pltpu.make_async_remote_copy(
-            src_ref=pks.at[kind, 0 if left else 1],
-            dst_ref=pkr.at[kind, 1 if left else 0],
+            src_ref=pks.at[kind, 0 if left else 1, body],
+            dst_ref=pkr.at[kind, 1 if left else 0, body],
             send_sem=col_send.at[kind, int(left)],
             recv_sem=col_recv.at[kind, int(left)],
             device_id={"gy": peer},
             device_id_type=MESH,
         )
 
-    has_left, has_right = gy > 0, gy < gy_n - 1
+    def corner_copy(kind, up, left):
+        which = 2 * int(up) + int(left)
+        return pltpu.make_async_remote_copy(
+            src_ref=pks.at[kind, 0 if left else 1, top if up else bottom],
+            dst_ref=pkr.at[kind, 1 if left else 0, below if up else above],
+            send_sem=corner_send.at[kind, which],
+            recv_sem=corner_recv.at[kind, which],
+            device_id=corner_id(up, left),
+            device_id_type=MESH,
+        )
 
     def plane(kind, p, t, at):
         if kind == 0:
@@ -205,16 +233,8 @@
     for kind in range(2):
         count = (6, 8)[kind]
 
-        @pl.when(has_down)
-        def _():
-            row_copy(kind, True).wait_recv()
-
-        @pl.when(has_up)
-        def _():
-            row_copy(kind, False).wait_recv()
-
         def pack(i, _):
-            at = pl.ds(pl.multiple_of(8 * i, 8), 8)
+            at = pl.ds(pl.multiple_of(HR + 8 * i, 8), 8)
             to_left = jnp.zeros((8, 128), F32)
             to_right = jnp.zeros((8, 128), F32)
             for p in range(count):
@@ -231,7 +251,7 @@
             pks[kind, 1, at, :] = to_right
             return 0
 
-        lax.fori_loop(0, blocks // 4, lambda i, x: [pack(4 * i + j, x) for j in range(4)][0], 0)
+        lax.fori_loop(0, rows // 32, lambda i, x: [pack(4 * i + j, x) for j in range(4)][0], 0)
 
         @pl.when(has_left)
         def _():
@@ -240,9 +260,29 @@
         @pl.when(has_right)
         def _():
             col_copy(kind, False).start()
+
+        for up, left in corners:
+
+            @pl.when(at_corner(up, left))
+            def _():
+                corner_copy(kind, up, left).start()
 
     def unpack(kind):
         count = (6, 8)[kind]
+
+        @pl.when(has_down)
+        def _():
+            row_copy(kind, True).wait_recv()
+
+        @pl.when(has_up)
+        def _():
+            row_copy(kind, False).wait_recv()
+
+        for up, left in corners:
+
+            @pl.when(at_corner(not up, not left))
+            def _():
+                corner_copy(kind, up, left).wait_recv()
 
         @pl.when(has_right)
         def _():
@@ -431,7 +471,7 @@
     acc = lax.fori_loop(0, CHUNKS, gram_chunk, jnp.zeros((2 * kk, 2 * kk), F32))
     acc = acc[:kk] + acc[kk:]
     gram = acc[:, :kk] + acc[:, kk:]
-    gram = jnp.concatenate([gram, jnp.zeros((kk, 128 - kk), F32)], axis=1)
+    gram = jnp.concatenate([gram[8 * g : 8 * g + 8] for g in range(nd)], axis=1)
 
     def reduce_copy(s, axis, index, count, o):
         return pltpu.make_async_remote_copy(
@@ -457,12 +497,29 @@
 
     line = lax.broadcasted_iota(jnp.int32, (kk, 128), 0)
     place = lax.broadcasted_iota(jnp.int32, (kk, 128), 1)
+    gram = [gram] + [pltpu.roll(gram, 128 - kk * g, axis=1) for g in range(1, nd)]
+    gram = jnp.where(place < kk, jnp.concatenate(gram, axis=0), 0.0)
     m = jnp.where(place == line + kk, 1.0, gram)
-    for k in range(kk - 1):
-        column = jnp.broadcast_to(m[:, k : k + 1], (kk, 128))
-        row = jnp.broadcast_to(m[k : k + 1, :], (kk, 128))
-        pivot = jnp.broadcast_to(column[k : k + 1, :], (kk, 128))
-        m = m - jnp.where(line > k, column, 0.0) * (row / pivot)
+
+    def wide(row):
+        return jnp.broadcast_to(row, (kk, 128))
+
+    for k in range(0, kk, 2):
+        col0 = jnp.broadcast_to(m[:, k : k + 1], (kk, 128))
+        col1 = jnp.broadcast_to(m[:, k + 1 : k + 2], (kk, 128))
+        row0, row1 = wide(m[k : k + 1, :]), wide(m[k + 1 : k + 2, :])
+        p00, p10 = wide(col0[k : k + 1, :]), wide(col0[k + 1 : k + 2, :])
+        p01, p11 = wide(col1[k : k + 1, :]), wide(col1[k + 1 : k + 2, :])
+        inv0 = 1.0 / p00
+        row0 = row0 * inv0
+        row1 = row1 - p10 * row0
+        over = p01 * inv0
+        inv1 = 1.0 / (p11 - p10 * over)
+        col1 = col1 - col0 * over
+        m = m - (
+            jnp.where(line > k, col0, 0.0) * row0
+            + jnp.where(line > k + 1, col1, 0.0) * (row1 * inv1)
+        )
     diag = jnp.sum(jnp.where(place == line, m, 0.0), axis=1, keepdims=True)
     m = m * lax.rsqrt(diag)
     upper_ref[...] = jnp.where(place >= line, m, 0.0)[:, :kk]
@@ -516,6 +573,12 @@
         @pl.when(has_down)
         def _():
             row_copy(kind, False).wait_send()
+
+        for up, left in corners:
+
+            @pl.when(at_corner(up, left))
+            def _():
+                corner_copy(kind, up, left).wait_send()
 
         @pl.when(has_left)
         def _():
@@ -579,14 +642,16 @@
             vmem((3, full, 6, 8, 128), F32),
             vmem((rows, 2, 8, 128), F32),
             vmem((nd, rows // nd, 2, 8, 128), F32),
-            vmem((3, kk, 128), F32),
-            vmem((3, most, kk, 128), F32),
+            vmem((3, 8, kk * nd), F32),
+            vmem((3, most, 8, kk * nd), F32),
             vmem((nd, CHUNKS, 2, 8, quarter, 128), F32),
             dma((14,)),
             dma((2, 2)),
             dma((2, 2)),
             dma((2, 2)),
             dma((2, 2)),
+            dma((2, 4)),
+            dma((2, 4)),
             dma((CHUNKS, nd)),
             dma((CHUNKS, nd)),
             dma((CHUNKS,)),

time: 100 us -> 98.5 us (0.985)
  the two profiles are of different devices: /device:TPU:64 before, /device:TPU:8 now
where the time goes in v4:
time: 98.5 us; the launch traced here: 98.3 us
  Pallas kernels  94.8 us (96%)
  local copies, waits for them, and re-layouts  2.88 us (3%)
    pallas_call x1, Pallas kernels, on_device(): pl.pallas_call(functools.partial(kernel, (gx_n, gy_n, nd, rows, total)),...  94.8 us
    unnamed x4, local copies, waits for them, and re-layouts  2.88 us

profile of v4, /device:TPU:8, one launch (start us, length us, event | category | flops | bytes accessed | tf_op | source)
XLA Modules:
  0.0 98.3 jit_solution(123594728010890074)
XLA Ops:
  0.6 94.8 %sketch.1 = (f32[8,128,256]{2,1,0:T(8,128)}, f32[32,32]{1,0:T(8,128)}) custom-call(f32[8,128,256]{2,1,0:T(8,128)} %dirs_hbm.1, f32[2,128,256]{2,1,0:T(8,128)} %vel_hbm.1, f32[128,256]{1,0:T(8,128)} %visc_hbm.1, f32[128,256]{1,0:T(8,128)} %drag_hbm.1, f32[128,256]{1,0:T(8,128)} %misfit_hbm.1, s32[128,256]{1,0:T(8,128)} %mask_hbm.1, s32[128,256]{1,0:T(8,128)} %ground_hbm.1), custom_call_target="tpu_custom_call" | custom-call | tf_op jit(solution)/shard_map/sketch/pallas_call | solution.py:620
  95.4 0.0 copy-start
  95.4 2.3 %copy.11 = f32[8,128,256]{2,1,0:T(8,128)} copy(f32[8,128,256]{2,1,0:T(8,128)} %get-tuple-element.4) | data formatting | bytes 2097152
  97.7 0.0 copy-done
  97.7 0.6 copy.12
Async XLA Ops:
  95.4 2.3 %copy-start = (f32[32,32]{1,0:T(8,128)S(1)}, f32[32,32]{1,0:T(8,128)}, u32[]{:S(2)}) copy-start(f32[32,32]{1,0:T(8,128)} %get-tuple-element.5) | copy-start | bytes 12292

commit v5 on v4

--- a/solution.py
+++ b/solution.py
@@ -193,16 +193,6 @@
             device_id_type=MESH,
         )
 
-    for kind in range(2):
-
-        @pl.when(has_up)
-        def _():
-            row_copy(kind, True).start()
-
-        @pl.when(has_down)
-        def _():
-            row_copy(kind, False).start()
-
     def col_copy(kind, left):
         peer = lax.rem(gy + (gy_n - 1 if left else 1), gy_n)
         return pltpu.make_async_remote_copy(
@@ -232,6 +222,14 @@
 
     for kind in range(2):
         count = (6, 8)[kind]
+
+        @pl.when(has_up)
+        def _():
+            row_copy(kind, True).start()
+
+        @pl.when(has_down)
+        def _():
+            row_copy(kind, False).start()
 
         def pack(i, _):
             at = pl.ds(pl.multiple_of(HR + 8 * i, 8), 8)
@@ -605,6 +603,21 @@
     lax.fori_loop(0, CHUNKS, finish, 0)
 
 
+def hand_over(basis_in, upper_in, basis_out, upper_out, held, held_upper, in_sem, out_sem):
+    count = basis_in.shape[0]
+    moves = [(basis_in.at[k], held.at[k], basis_out.at[k]) for k in range(count)]
+    moves.append((upper_in, held_upper, upper_out))
+    takes = [pltpu.make_async_copy(a, h, in_sem.at[i]) for i, (a, h, _) in enumerate(moves)]
+    gives = [pltpu.make_async_copy(h, b, out_sem.at[i]) for i, (_, h, b) in enumerate(moves)]
+    for c in takes:
+        c.start()
+    for take, give in zip(takes, gives):
+        take.wait()
+        give.start()
+    for c in gives:
+        c.wait()
+
+
 def on_device(mesh, directions, velocity, viscosity, basal_drag, misfit_weight, ice_mask, grounded):
     gx_n, gy_n, nd = (mesh.shape[a] for a in ("gx", "gy", "dir"))
     own, rows, cols = directions.shape
@@ -617,7 +630,7 @@
     any_space = pl.BlockSpec(memory_space=pl.ANY)
     dma = pltpu.SemaphoreType.DMA
     vmem = pltpu.VMEM
-    return pl.pallas_call(
+    basis, upper = pl.pallas_call(
         functools.partial(kernel, (gx_n, gy_n, nd, rows, total)),
         out_shape=(
             jax.ShapeDtypeStruct((own, rows, cols), F32),
@@ -666,6 +679,23 @@
         ),
         name="sketch",
     )(directions, velocity, viscosity, basal_drag, misfit_weight, ice_mask, grounded)
+    return pl.pallas_call(
+        hand_over,
+        out_shape=(
+            jax.ShapeDtypeStruct((own, rows, cols), F32),
+            jax.ShapeDtypeStruct((kk, kk), F32),
+        ),
+        in_specs=[any_space] * 2,
+        out_specs=(any_space, any_space),
+        scratch_shapes=[
+            vmem((own, rows, cols), F32),
+            vmem((kk, kk), F32),
+            dma((own + 1,)),
+            dma((own + 1,)),
+        ],
+        compiler_params=pltpu.CompilerParams(vmem_limit_bytes=62 << 20),
+        name="hand_over",
+    )(basis, upper)
 
 
 def solution(mesh):

time: 98.5 us -> 94.8 us (0.962)
  the two profiles are of different devices: /device:TPU:8 before, /device:TPU:33 now
where the time goes in v5:
time: 94.8 us; the launch traced here: 94.6 us
  Pallas kernels  94 us (99%)
    pallas_call x1, Pallas kernels, on_device(): pl.pallas_call(functools.partial(kernel, (gx_n, gy_n, nd, rows, total)),...  91.9 us
    pallas_call x1, Pallas kernels, on_device(): pl.pallas_call(hand_over, out_shape=(jax.ShapeDtypeStruct((own, rows, col...  2.11 us

profile of v5, /device:TPU:33, one launch (start us, length us, event | category | flops | bytes accessed | tf_op | source)
XLA Modules:
  0.0 94.6 jit_solution(2380979398132113006)
XLA Ops:
  0.6 91.9 %sketch.1 = (f32[8,128,256]{2,1,0:T(8,128)}, f32[32,32]{1,0:T(8,128)}) custom-call(f32[8,128,256]{2,1,0:T(8,128)} %dirs_hbm.1, f32[2,128,256]{2,1,0:T(8,128)} %vel_hbm.1, f32[128,256]{1,0:T(8,128)} %visc_hbm.1, f32[128,256]{1,0:T(8,128)} %drag_hbm.1, f32[128,256]{1,0:T(8,128)} %misfit_hbm.1, s32[128,256]{1,0:T(8,128)} %mask_hbm.1, s32[128,256]{1,0:T(8,128)} %ground_hbm.1), custom_call_target="tpu_custom_call" | custom-call | tf_op jit(solution)/shard_map/sketch/pallas_call | solution.py:633
  92.5 2.1 %hand_over.1 = (f32[8,128,256]{2,1,0:T(8,128)}, f32[32,32]{1,0:T(8,128)}) custom-call(f32[8,128,256]{2,1,0:T(8,128)} %get-tuple-element.4.basis_in, f32[32,32]{1,0:T(8,128)} %get-tuple-element.5.upper_in), custom_call_target="tpu_custom_call" | custom-call | tf_op jit(solution)/shard_map/hand_over/pallas_call | solution.py:682

commit v6 on v5

--- a/solution.py
+++ b/solution.py
@@ -156,20 +156,6 @@
     def _():
         pkr[:, 1] = jnp.zeros((2, full, 128), F32)
 
-    cols = 256
-    k_in = lax.broadcasted_iota(jnp.int32, (384, 384), 0)
-    k_out = lax.broadcasted_iota(jnp.int32, (384, 384), 1)
-    inside = jnp.where(k_in < cols + HC, k_in + HC, jnp.where(k_in >= 384 - HC, k_in - (384 - HC), -1))
-    third = (k_out % 128) * 3 + k_out // 128
-    there = jnp.where(inside == third, 1.0, 0.0).astype(BF16)
-    spread[0:384] = there
-    spread[384:768] = there
-    k_in = lax.broadcasted_iota(jnp.int32, (384, cols), 0)
-    k_out = lax.broadcasted_iota(jnp.int32, (384, cols), 1)
-    back = jnp.where((k_in % 128) * 3 + k_in // 128 == k_out + HC, 1.0, 0.0).astype(BF16)
-    gather[0:384] = back
-    gather[384:768] = back
-
     for c in copies:
         c.wait()
     for t in range(2):
@@ -312,7 +298,7 @@
             return 0
 
         lax.fori_loop(0, full // 32, lambda i, x: [one(2 * i + j, x) for j in range(2)][0], 0)
-        size = 2 * full
+        size = count // 2 * full
 
         def spread_out(i, _):
             part = halves[pl.ds(pl.multiple_of(6 * kind * full + i * size, 16), size), :]
@@ -322,7 +308,21 @@
                 ref[t, pl.ds(pl.multiple_of(i * size, 8), size), :] = out[:, 128 * t : 128 * t + 128]
             return 0
 
-        lax.fori_loop(0, count // 2, spread_out, 0)
+        lax.fori_loop(0, 2, spread_out, 0)
+
+    cols = 256
+    k_in = lax.broadcasted_iota(jnp.int32, (384, 384), 0)
+    k_out = lax.broadcasted_iota(jnp.int32, (384, 384), 1)
+    inside = jnp.where(k_in < cols + HC, k_in + HC, jnp.where(k_in >= 384 - HC, k_in - (384 - HC), -1))
+    third = (k_out % 128) * 3 + k_out // 128
+    there = jnp.where(inside == third, 1.0, 0.0).astype(BF16)
+    spread[0:384] = there
+    spread[384:768] = there
+    k_in = lax.broadcasted_iota(jnp.int32, (384, cols), 0)
+    k_out = lax.broadcasted_iota(jnp.int32, (384, cols), 1)
+    back = jnp.where((k_in % 128) * 3 + k_in // 128 == k_out + HC, 1.0, 0.0).astype(BF16)
+    gather[0:384] = back
+    gather[384:768] = back
 
     unpack(0)
 

time: 94.8 us -> 94.1 us (level)
  the two profiles are of different devices: /device:TPU:33 before, /device:TPU:64 now
where the time goes in v6:
time: 94.1 us; the launch traced here: 92.6 us
  Pallas kernels  92 us (98%)
    pallas_call x1, Pallas kernels, on_device(): pl.pallas_call(functools.partial(kernel, (gx_n, gy_n, nd, rows, total)),...  89.9 us
    pallas_call x1, Pallas kernels, on_device(): pl.pallas_call(hand_over, out_shape=(jax.ShapeDtypeStruct((own, rows, col...  2.11 us

profile of v6, /device:TPU:64, one launch (start us, length us, event | category | flops | bytes accessed | tf_op | source)
XLA Modules:
  0.0 92.6 jit_solution(6655002664110030248)
XLA Ops:
  0.6 89.9 %sketch.1 = (f32[8,128,256]{2,1,0:T(8,128)}, f32[32,32]{1,0:T(8,128)}) custom-call(f32[8,128,256]{2,1,0:T(8,128)} %dirs_hbm.1, f32[2,128,256]{2,1,0:T(8,128)} %vel_hbm.1, f32[128,256]{1,0:T(8,128)} %visc_hbm.1, f32[128,256]{1,0:T(8,128)} %drag_hbm.1, f32[128,256]{1,0:T(8,128)} %misfit_hbm.1, s32[128,256]{1,0:T(8,128)} %mask_hbm.1, s32[128,256]{1,0:T(8,128)} %ground_hbm.1), custom_call_target="tpu_custom_call" | custom-call | tf_op jit(solution)/shard_map/sketch/pallas_call | solution.py:633
  90.5 2.1 %hand_over.1 = (f32[8,128,256]{2,1,0:T(8,128)}, f32[32,32]{1,0:T(8,128)}) custom-call(f32[8,128,256]{2,1,0:T(8,128)} %get-tuple-element.4.basis_in, f32[32,32]{1,0:T(8,128)} %get-tuple-element.5.upper_in), custom_call_target="tpu_custom_call" | custom-call | tf_op jit(solution)/shard_map/hand_over/pallas_call | solution.py:682
